TPU v7x, 256 devices: a whole 4x4x8 slice. The times are simulated.
256 devices in a mesh: dp: 8 (over y, x_hi), mp: 32 (over z, x_lo, core).
Axes of the slice: x: 4 (x_hi: 2, x_lo: 2; x = x_hi * 2 + x_lo), y: 4, z: 8, core: 2. Of those that a mesh axis runs over, the one named last changes fastest.
Arguments:
- activations: bfloat16 [4096, 4096], P('dp', 'mp'), may hold values from -22 to 22
- out_grads: bfloat16 [4096, 32768], P('dp', 'mp'), may hold values from -1 to 1
- weight: float32 [4096, 32768], P('dp', 'mp'), may hold values from -0.09375 to 0.09375
- row_state: float32 [4096], P('dp'), may hold values from 0.1 to 1.6
- column_state: float32 [32768], P('mp'), may hold values from 0.1 to 1.6
- next_batch: bfloat16 [4096, 4096], P('dp', 'mp'), may hold values from -6 to 6
Outputs:
- new_weight: float32 [4096, 32768], P('dp', 'mp')
- update: float32 [4096, 32768], P('dp', 'mp')
- row_moment: float32 [4096], P('dp')
- column_moment: float32 [32768], P('mp')
- next_hidden: bfloat16 [4096, 32768], P('dp', 'mp')
All inputs are finite; a program needn't handle non-finite values.
Results may differ from a plain program's by a relative error of at most 0.001.
The roundings to bfloat16 on the way count: a program that leaves them out, or rounds other values in their place, can miss the bound.
Values may be sent and summed in bfloat16 or wider, within the bound.
A program may use at most 128 MiB of HBM per device.

v0:
```python
import jax
import jax.numpy as jnp
from jax import lax
from jax.sharding import PartitionSpec as P

D = 4096
FF = 32768


tiny_square = 1e-30
weight_eps = 1e-06
decay_rate = 0.5
clip_level = 0.5
learn_rate = 0.01


def body(activations, out_grads, weight, row_state, column_state, next_batch):
    features, next_features = (
        lax.all_gather(activations, "mp", axis=1, tiled=True),
        lax.all_gather(next_batch, "mp", axis=1, tiled=True),
    )
    contract = (((0,), (0,)), ((), ()))
    block = features
    gradient = lax.psum_scatter(
        lax.dot_general(block, out_grads, contract, preferred_element_type=jnp.float32),
        "dp",
        scatter_dimension=0,
        tiled=True,
    )
    squares = gradient * gradient + tiny_square
    row_part = jnp.sum(squares, axis=1)
    column_part = jnp.sum(squares, axis=0)
    row_sum = lax.psum(row_part, "mp")
    column_sum = lax.psum(column_part, "dp")
    row_moment = decay_rate * row_state + (1.0 - decay_rate) * (row_sum / FF)
    column_moment = decay_rate * column_state + (1.0 - decay_rate) * (column_sum / D)
    raw_update = gradient * lax.rsqrt(row_moment[:, None] * column_moment[None, :])
    raw_total, weight_total = lax.psum(
        (jnp.sum(raw_update * raw_update), jnp.sum(weight * weight)), ("dp", "mp")
    )
    rms_update = jnp.sqrt(raw_total / (D * FF))
    update = raw_update / jnp.maximum(1.0, rms_update / clip_level)
    rms_weight = jnp.sqrt(weight_total / (D * FF) + weight_eps)
    new_weight = weight - learn_rate * rms_weight * update
    weight_half = new_weight.astype(jnp.bfloat16)
    block = next_features
    hidden_sum = jnp.dot(
        block,
        lax.all_gather(weight_half, "dp", axis=0, tiled=True),
        preferred_element_type=jnp.float32,
    )
    return (new_weight, update, row_moment, column_moment, hidden_sum.astype(jnp.bfloat16))


def solution(mesh):
    return jax.shard_map(
        body,
        mesh=mesh,
        in_specs=(P("dp", "mp"), P("dp", "mp"), P("dp", "mp"), P("dp"), P("mp"), P("dp", "mp")),
        out_specs=(P("dp", "mp"), P("dp", "mp"), P("dp"), P("mp"), P("dp", "mp")),
        check_vma=False,
    )
```

profile of v0, /device:TPU:6, one launch (start us, length us, event | category | flops | bytes accessed | tf_op | source)
XLA Modules:
  0.0 576.0 jit_solution(11072777842069617354)
XLA Ops:
  7.2 0.0 copy-start
  7.2 0.0 all-gather.4.cloned.1.call-start
  7.2 0.7 all-gather.4.cloned.1.call-update
  7.9 0.0 reduce-scatter.2.cloned.1.call-start
  8.0 77.3 %all-gather.4.cloned.1.call-done = bf16[512,4096]{1,0:T(8,128)(2,1)} async-done(((bf16[512,128]{1,0:T(8,128)(2,1)}), bf16[512,4096]{1,0:T(8,128)(2,1)}) %all-gather.4.cloned.1.call-update) | async-done | bytes 4194320 | tf_op jit(solution)/shard_map/all_gather | solution.py:19
  85.2 0.0 copy-done
  85.3 10.4 %fusion.6 = f32[4096,1024]{1,0:T(8,128)} fusion(bf16[512,4096]{1,0:T(8,128)(2,1)} %all-gather.4.cloned.1.call-done, bf16[512,1024]{1,0:T(8,128)(2,1)S(1)} %copy-done), kind=kOutput, calls=%fused_computation.13 | convolution fusion | flops 4294967296 | bytes 22020096 | tf_op jit(solution)/shard_map/dot_general | solution.py:25
  95.6 0.0 copy-start.2
  95.6 0.0 reduce-scatter.2.cloned.1.call-update
  95.6 0.0 all-gather.8.cloned.1.call-start
  95.7 0.7 all-gather.8.cloned.1.call-update
  96.4 0.0 copy-start.6
  96.4 0.0 copy-start.5
  96.4 0.0 all-gather.6.cloned.1.call-start
  96.5 0.8 copy-done.2
  97.2 1.1 multiply_reduce_fusion.1
  98.4 194.5 %reduce-scatter.2.cloned.1.call-done = f32[512,1024]{1,0:T(8,128)} async-done(((f32[4096,1024]{1,0:T(8,128)}), f32[512,1024]{1,0:T(8,128)}) %reduce-scatter.2.cloned.1.call-update) | async-done | bytes 2097168 | tf_op jit(solution)/shard_map/reduce_scatter | solution.py:24
  292.9 0.0 copy-start.1
  292.9 2.1 fusion.1
  295.0 50.4 %psum.29 = f32[512]{0:T(512)S(1)} all-reduce(f32[512]{0:T(512)S(1)} %get-tuple-element.10), channel_id=1, replica_groups=mesh['dp'=8,'mp'=32] {'mp'}, use_global_device_ids=true, to_apply=%region_4.0 | all-reduce | flops 512 | bytes 4096 | tf_op jit(solution)/shard_map/psum | solution.py:33
  345.4 20.2 %psum.30 = f32[1024]{0:T(1024)S(1)} all-reduce(f32[1024]{0:T(1024)S(1)} %get-tuple-element.11), channel_id=1, replica_groups=mesh['dp'=8,'mp'=32] {'dp'}, use_global_device_ids=true, to_apply=%region_6.0 | all-reduce | flops 1024 | bytes 8192 | tf_op jit(solution)/shard_map/psum | solution.py:34
  365.7 0.0 copy-done.6
  365.7 0.0 copy-done.5
  365.7 0.0 copy-start.4
  365.7 0.0 copy-done.1
  365.7 0.0 copy-start.3
  365.8 1.5 multiply_reduce_fusion
  367.2 78.4 %all-reduce = (f32[]{:T(128)}, f32[]{:T(128)}) all-reduce(f32[]{:T(128)} %multiply_reduce_fusion, f32[]{:T(128)} %multiply_reduce_fusion.1), channel_id=1, replica_groups=mesh['dp'=8,'mp'=32] {'dp','mp'}, use_global_device_ids=true, to_apply=%region_8.0 | all-reduce | flops 2 | bytes 16 | tf_op jit(solution)/shard_map/psum | solution.py:38
  447.0 4.5 fusion.4
  451.5 0.0 copy-done.4
  451.5 0.0 copy-done.3
  451.5 0.0 all-gather.6.cloned.1.call-update
  451.5 0.0 all-gather.8.cloned.1.call-done
  451.5 107.5 %all-gather.6.cloned.1.call-done = bf16[4096,1024]{1,0:T(8,128)(2,1)} async-done(((bf16[512,1024]{1,0:T(8,128)(2,1)}), bf16[4096,1024]{1,0:T(8,128)(2,1)}) %all-gather.6.cloned.1.call-update) | async-done | bytes 8388624 | tf_op jit(solution)/shard_map/all_gather | solution.py:49
  559.0 9.1 %fusion.3 = bf16[512,1024]{0,1:T(8,128)(2,1)S(1)} fusion(bf16[4096,1024]{1,0:T(8,128)(2,1)} %all-gather.6.cloned.1.call-done, bf16[512,4096]{1,0:T(8,128)(2,1)} %all-gather.8.cloned.1.call-done), kind=kOutput, calls=%fused_computation.9 | convolution fusion | flops 4295491584 | bytes 13631488 | tf_op jit(solution)/shard_map/dot_general | solution.py:47
  568.1 1.3 copy.11
  (2 shorter events, 0.0 us)
Async XLA Ops:
  7.2 78.1 %copy-start = (bf16[512,1024]{1,0:T(8,128)(2,1)S(1)}, bf16[512,1024]{1,0:T(8,128)(2,1)}, u32[]{:S(2)}) copy-start(bf16[512,1024]{1,0:T(8,128)(2,1)} %param.7) | copy-start | bytes 3145732
  7.2 78.1 %all-gather.4.cloned.1.call-start = ((), (), s32[]{:S(2)}) async-start(), calls=%async_computation.1 | async-start | bytes 4325376 | tf_op jit(solution)/shard_map/all_gather | solution.py:19
  7.9 284.9 %reduce-scatter.2.cloned.1.call-start = ((), (), s32[]{:S(2)}) async-start(), calls=%async_computation.2 | async-start | bytes 18874368 | tf_op jit(solution)/shard_map/reduce_scatter | solution.py:24
  95.6 1.6 copy-start.2
  95.6 355.9 %all-gather.8.cloned.1.call-start = ((), (), s32[]{:S(2)}) async-start(), calls=%async_computation.4 | async-start | bytes 4325376 | tf_op jit(solution)/shard_map/all_gather | solution.py:20
  96.4 269.3 %copy-start.6 = (f32[512]{0:T(512)S(1)}, f32[512]{0:T(512)}, u32[]{:S(2)}) copy-start(f32[512]{0:T(512)} %param.9) | copy-start | bytes 6148
  96.4 269.3 %copy-start.5 = (f32[1024]{0:T(1024)S(1)}, f32[1024]{0:T(1024)}, u32[]{:S(2)}) copy-start(f32[1024]{0:T(1024)} %param.10) | copy-start | bytes 12292
  96.4 462.6 %all-gather.6.cloned.1.call-start = ((), (), s32[]{:S(2)}) async-start(), calls=%async_computation.3 | async-start | bytes 9437184 | tf_op jit(solution)/shard_map/all_gather | solution.py:49
  292.9 72.9 %copy-start.1 = (f32[512,1024]{1,0:T(8,128)S(1)}, f32[512,1024]{1,0:T(8,128)}, u32[]{:S(2)}) copy-start(f32[512,1024]{1,0:T(8,128)} %reduce-scatter.2.cloned.1.call-done) | copy-start | bytes 6291460
  365.7 85.8 %copy-start.4 = (f32[512]{0:T(512)}, f32[512]{0:T(512)S(1)}, u32[]{:S(2)}) copy-start(f32[512]{0:T(512)S(1)} %multiply_add_fusion.2) | copy-start | bytes 6148
  365.7 85.7 %copy-start.3 = (f32[1024]{0:T(1024)}, f32[1024]{0:T(1024)S(1)}, u32[]{:S(2)}) copy-start(f32[1024]{0:T(1024)S(1)} %multiply_add_fusion.1) | copy-start | bytes 12292
Sparse Core Ops, SparseCore 0:
  9.8 75.4 all-gather.3
  95.8 197.0 reduce-scatter.1
  294.6 72.2 all-gather.7
  451.6 107.3 all-gather.5
where the time goes:
time: 578 us; the launch traced here: 576 us
  waiting for transfers between devices  381 us (66%)
  blocking collectives  149 us (26%)
  matrix products  19.5 us (3%)
  between operations  15.2 us (3%)
  other arithmetic  9.27 us (2%)
    reduce_scatter x1, waiting for transfers between devices, body(): lax.psum_scatter(lax.dot_general(block, out_grads, contract, preferred_el...  195 us
    all_gather x1, waiting for transfers between devices, body(): lax.all_gather(weight_half, 'dp', axis=0, tiled=True)  107 us
    psum x1, blocking collectives, body(): lax.psum((jnp.sum(raw_update * raw_update), jnp.sum(weight * weight)), ('...  78.4 us
    all_gather x1, waiting for transfers between devices, body(): lax.all_gather(activations, 'mp', axis=1, tiled=True)  77.3 us
    psum x1, blocking collectives, body(): row_sum = lax.psum(row_part, 'mp')  50.4 us
    psum x1, blocking collectives, body(): column_sum = lax.psum(column_part, 'dp')  20.2 us
  transfers between devices with their start and end apart: 4, of which 3 were waited for; matrix products, arithmetic and copies ran while one was open for 2% of the time, Pallas kernels for 0%

commit v1 on v0

v1 whole, which is shorter than its diff:
```python
import functools
import heapq

import jax
import jax.numpy as jnp
from jax import lax
from jax.experimental import pallas as pl
from jax.experimental.pallas import tpu as pltpu
from jax.sharding import PartitionSpec as P

D = 4096
FF = 32768

tiny_square = 1e-30
weight_eps = 1e-06
decay_rate = 0.5
clip_level = 0.5
learn_rate = 0.01

ROWS = 512
COLS = 1024
W = 128
CHUNKS = COLS // W
Y_FIRST = (0, 1, 2)
X_FIRST = (3, 4, 5, 6, 7)
COPIES = 400
RELAYS = 2 * (len(X_FIRST) + 4 * len(Y_FIRST))

HOP_US = 1.7
RATE = 46e3
DOT_US = 1.6

F32 = jnp.float32
BF16 = jnp.bfloat16
MESH = pl.DeviceIdType.MESH


class Place:
    def __init__(self):
        self.dp = lax.axis_index("dp")
        self.mp = lax.axis_index("mp")
        self.y = self.dp // 2
        self.xh = self.dp % 2
        self.z = self.mp // 4
        self.xl = (self.mp // 2) % 2
        self.core = self.mp % 2
        self.x = 2 * self.xh + self.xl

    def device(self, dy=0, dx=0, dz=0, dcore=0):
        y = (self.y + dy) % 4
        x = (self.x + dx) % 4
        z = (self.z + dz) % 8
        core = (self.core + dcore) % 2
        return (2 * y + x // 2, 4 * z + 2 * (x % 2) + core)


class Net:
    def __init__(self, send_sems, recv_sems):
        self.send_sems, self.recv_sems = send_sems, recv_sems
        self.copies, self.heap, self.free = [], [], {}
        self.now = 0.0
        self.first = 0

    def send(self, link, src, dst, device, size, then, hop=HOP_US):
        k = len(self.copies)
        copy = pltpu.make_async_remote_copy(
            src_ref=src, dst_ref=dst, send_sem=self.send_sems.at[k], recv_sem=self.recv_sems.at[k],
            device_id=device, device_id_type=MESH)
        copy.start()
        self.copies.append(copy)
        begin = max(self.free.get(link, 0.0), self.now)
        end = begin + size / (RATE * (12 if link == "core" else 1))
        self.free[link] = end
        heapq.heappush(self.heap, (end + hop, k, copy, then))

    def run(self, until=None):
        while self.heap and not (until and until()):
            at, _, copy, then = heapq.heappop(self.heap)
            self.now = max(self.now, at)
            copy.wait_recv()
            if then is not None:
                then()

    def finish(self):
        for copy in self.copies[self.first:]:
            copy.wait_send()
        self.first = len(self.copies)


def block(ref, c, t, half=None):
    if half is None:
        return ref.at[c, pl.ds(pl.multiple_of(t * ROWS, ROWS), ROWS), :]
    rows = ROWS // 2
    return ref.at[c, pl.ds(pl.multiple_of(t * ROWS + half * rows, rows), rows), :]


class GatherDp:
    FULL = ROWS * W * 2

    def __init__(self, net, me, buf, relay, done):
        self.net, self.me, self.buf, self.relay, self.done = net, me, buf, relay, done
        self.left = {c: 10 for c in X_FIRST}
        self.left.update({c: 12 for c in Y_FIRST})
        self.relays = 0
        self.partner_halves = {c: 0 for c in X_FIRST}

    def index(self, dy, other):
        xh = (self.me.xh + 1) % 2 if other else self.me.xh
        return 2 * ((self.me.y + dy) % 4) + xh

    def got(self, c):
        self.left[c] -= 1
        if self.left[c] == 0:
            self.done(c)

    def along_y(self, c, other):
        for sign in (1, -1):
            part = block(self.buf, c, self.index(0, other))
            self.net.send(("y", sign), part, part, self.me.device(dy=sign), self.FULL,
                          functools.partial(self.from_y, c, other, sign))

    def from_y(self, c, other, sign):
        half = 0 if sign == 1 else 1
        part = block(self.buf, c, self.index(-sign, other), half)
        self.net.send(("y", sign), part, part, self.me.device(dy=sign), self.FULL // 2,
                      functools.partial(self.from_far_y, c, other, half))
        if c in Y_FIRST:
            self.along_x(c, -sign, 0)
            self.along_x(c, -sign, 1)
        self.got(c)

    def from_far_y(self, c, other, half):
        if c in Y_FIRST:
            self.along_x(c, 2, half)
        self.got(c)

    def along_x(self, c, dy, half):
        sign = 1 if half == 0 else -1
        slot = self.relay.at[self.relays]
        self.relays += 1
        self.net.send(("x", sign), block(self.buf, c, self.index(dy, False), half), slot,
                      self.me.device(dx=sign), self.FULL // 2,
                      functools.partial(self.relayed, c, dy, half, sign, slot))

    def relayed(self, c, dy, half, sign, slot):
        xh = ((self.me.x + 4 - sign) % 4) // 2
        t = 2 * ((self.me.y + dy) % 4) + xh
        self.net.send(("x", sign), slot, block(self.buf, c, t, half), self.me.device(dx=sign),
                      self.FULL // 2, functools.partial(self.from_x, c))

    def from_x(self, c):
        if c in X_FIRST:
            self.partner_halves[c] += 1
            if self.partner_halves[c] == 2:
                self.along_y(c, True)
        self.got(c)


class GatherMp:
    SIZE = ROWS * W * 2

    def __init__(self, net, me, strip, reach, done):
        self.net, self.me, self.strip, self.reach, self.done = net, me, strip, reach, done
        self.left = 31

    def got(self):
        self.left -= 1
        if self.left == 0:
            self.done()

    def place(self, dz, other):
        xl = (self.me.xl + 1) % 2 if other else self.me.xl
        return self.strip((self.me.z + dz) % 8, xl, self.me.core)

    def start(self):
        mine = self.place(0, False)
        dp, z, xl, core = self.me.dp, self.me.z, (self.me.xl + 1) % 2, self.me.core
        self.net.send(("x", 0), mine, mine, (dp, 4 * z + 2 * xl + core), self.SIZE, self.pair)
        self.have(0, False)

    def pair(self):
        self.have(0, True)
        self.got()

    def have(self, dz, other):
        part = self.place(dz, other)
        for sign in (1, -1):
            hops = -dz * sign
            if (dz == 0 or hops > 0) and hops < self.reach[sign]:
                self.net.send(("z", sign), part, part, self.me.device(dz=sign), self.SIZE,
                              functools.partial(self.from_z, dz - sign, other))
        self.net.send("core", part, part, self.me.device(dcore=1), self.SIZE, self.got, hop=1.0)

    def from_z(self, dz, other):
        self.have(dz, other)
        self.got()


def kernel(act, out_grads, weight, row_state, col_state, nxt,
           new_weight, update, row_out, col_out, hidden,
           act_v, nxt_v, act_t, pieces, at, xb, ob, wb, o_relay, w_relay,
           w_v, g_v, u_v, h_v, colbuf, rowbuf, tbuf, lastbuf,
           send_sems, recv_sems, a_send, a_recv, b_send, b_recv,
           col_send, col_recv, row_send, row_recv, t_send, t_recv, last_send, last_recv, local_sems):
    me = Place()
    dp, mp = me.dp, me.mp

    loads = [
        pltpu.make_async_copy(act, act_v, local_sems.at[0]),
        pltpu.make_async_copy(nxt, xb.at[:, pl.ds(pl.multiple_of(mp * W, W), W)], local_sems.at[1]),
        pltpu.make_async_copy(weight, w_v, local_sems.at[2]),
    ]
    for c in range(CHUNKS):
        loads.append(pltpu.make_async_copy(
            out_grads.at[:, pl.ds(c * W, W)], block(ob, c, dp), local_sems.at[3 + c]))
    for copy in loads:
        copy.start()

    barrier = pltpu.get_barrier_semaphore()

    def greet_mp(k, carry):
        pl.semaphore_signal(barrier, inc=1, device_id=(dp, (mp + k) % 32), device_id_type=MESH)
        return carry

    def greet_dp(k, carry):
        pl.semaphore_signal(barrier, inc=1, device_id=((dp + k) % 8, mp), device_id_type=MESH)
        return carry

    lax.fori_loop(1, 32, greet_mp, 0)
    lax.fori_loop(1, 8, greet_dp, 0)
    pl.semaphore_signal(barrier, inc=1, device_id=me.device(dx=2 * me.xl - 1), device_id_type=MESH)

    loads[0].wait()
    act_t[...] = act_v[...].T
    pieces[me.z] = act_t[pl.ds(pl.multiple_of(16 * me.z, 16), 16), :]
    pl.semaphore_wait(barrier, 39)

    def to_z(k):
        z = (me.z + k) % 8
        return pltpu.make_async_remote_copy(
            src_ref=act_t.at[pl.ds(pl.multiple_of(16 * z, 16), 16), :], dst_ref=pieces.at[me.z],
            send_sem=a_send.at[k], recv_sem=a_recv.at[k],
            device_id=(dp, (mp + 4 * k) % 32), device_id_type=MESH)

    strip_row = pl.multiple_of((2 * me.xl + me.core) * W + 16 * me.z, 16)

    def to_dp(k):
        i = (dp + k) % 8
        return pltpu.make_async_remote_copy(
            src_ref=pieces.at[i],
            dst_ref=at.at[pl.ds(strip_row, 16), pl.ds(pl.multiple_of(dp * ROWS, ROWS), ROWS)],
            send_sem=b_send.at[k], recv_sem=b_recv.at[k],
            device_id=(i, mp), device_id_type=MESH)

    for k in range(1, 8):
        to_z(k).start()

    net = Net(send_sems, recv_sems)
    state = {"at": False, "ready": [], "count": 0}
    colbuf_row = colbuf.at[dp]

    def product(left, right, c, out):
        out[...] = jnp.zeros_like(out)

        def step(k, carry):
            s = pl.multiple_of(k * 512, 512)
            out[...] += jnp.dot(left[:, pl.ds(s, 512)], right[c, pl.ds(s, 512), :],
                                preferred_element_type=F32)
            return carry

        lax.fori_loop(0, 8, step, 0)

    def gradient(c):
        net.now += DOT_US
        product(at, ob, c, g_v.at[c])
        squares = g_v[c] * g_v[c] + tiny_square
        colbuf_row[:, pl.ds(c * W, W)] = jnp.sum(squares, axis=0, keepdims=True)
        if state["count"] == 0:
            h_v[...] = squares
        else:
            h_v[...] += squares
        state["count"] += 1

    def chunk_here(c):
        if state["at"]:
            gradient(c)
        else:
            state["ready"].append(c)

    def at_here():
        state["at"] = True
        for c in state["ready"]:
            gradient(c)

    first = GatherDp(net, me, ob, o_relay, chunk_here)
    for c in Y_FIRST:
        loads[3 + c].wait()
        first.along_y(c, False)
        first.along_x(c, 0, 0)
        first.along_x(c, 0, 1)
    for k in range(1, 8):
        to_z(k).wait_recv()
    for k in range(1, 8):
        to_dp(k).start()
    at[pl.ds(strip_row, 16), pl.ds(pl.multiple_of(dp * ROWS, ROWS), ROWS)] = pieces[dp]
    net.now = 5.0
    for c in X_FIRST:
        loads[3 + c].wait()
        first.along_x(c, 0, 0)
        first.along_x(c, 0, 1)
        first.along_y(c, False)

    def strip_x(z, xl, core):
        return xb.at[:, pl.ds(pl.multiple_of((4 * z + 2 * xl + core) * W, W), W)]

    def strip_a(z, xl, core):
        return at.at[pl.ds(pl.multiple_of((2 * xl + core) * W + 16 * z, 16), 16), :]

    for k in range(1, 8):
        to_dp(k).wait_recv()
    GatherMp(net, me, strip_a, {1: 4, -1: 3}, at_here).start()
    loads[1].wait()
    GatherMp(net, me, strip_x, {1: 3, -1: 4}, lambda: None).start()

    loads[2].wait()
    wsq = jnp.zeros((8, 128), F32)

    def weight_step(k, carry):
        w = w_v[pl.ds(pl.multiple_of(k * 8, 8), 8), :]
        w = w * w
        for c in range(CHUNKS):
            carry = carry + w[:, c * W:(c + 1) * W]
        return carry

    wsq = lax.fori_loop(0, ROWS // 8, weight_step, wsq)
    wsum = jnp.sum(wsq, axis=0, keepdims=True)

    net.run()

    def to_all(buf, mine, axis, size, send, recv):
        def copy(k):
            device = ((mine + k) % size, mp) if axis == "dp" else (dp, (mine + k) % size)
            return pltpu.make_async_remote_copy(
                src_ref=buf.at[mine], dst_ref=buf.at[mine], send_sem=send.at[k], recv_sem=recv.at[k],
                device_id=device, device_id_type=MESH)

        def start(k, carry):
            copy(k).start()
            return carry

        def wait(k, carry):
            copy(k).wait_recv()
            return carry

        def wait_sent(k, carry):
            copy(k).wait_send()
            return carry

        return (lambda: lax.fori_loop(1, size, start, 0), lambda: lax.fori_loop(1, size, wait, 0),
                lambda: lax.fori_loop(1, size, wait_sent, 0))

    col_start, col_wait, col_sent = to_all(colbuf, dp, "dp", 8, col_send, col_recv)
    row_start, row_wait, row_sent = to_all(rowbuf, mp, "mp", 32, row_send, row_recv)
    t_start, t_wait, t_sent = to_all(tbuf, mp, "mp", 32, t_send, t_recv)
    last_start, last_wait, last_sent = to_all(lastbuf, dp, "dp", 8, last_send, last_recv)

    col_start()
    my_row = rowbuf.at[mp]
    my_row[:, :ROWS] = jnp.sum(h_v[...].T, axis=0, keepdims=True)
    my_row[:, ROWS:] = wsum
    row_start()
    col_wait()
    column_moment = decay_rate * col_state[...] + (1.0 - decay_rate) * (
        jnp.sum(colbuf[...], axis=0) / D)
    col_out[...] = column_moment
    inverse = 1.0 / column_moment
    for c in range(CHUNKS):
        term = g_v[c] * g_v[c] * inverse[:, c * W:(c + 1) * W]
        if c == 0:
            h_v[...] = term
        else:
            h_v[...] += term
    my_t = tbuf.at[mp]
    my_t[...] = jnp.sum(h_v[...].T, axis=0, keepdims=True)
    t_start()
    row_wait()
    rows = jnp.sum(rowbuf[...], axis=0)
    row_moment = decay_rate * row_state[...] + (1.0 - decay_rate) * (rows[:, :ROWS] / FF)
    row_out[...] = row_moment
    t_wait()
    terms = jnp.sum(tbuf[...], axis=0) / row_moment
    last = lastbuf.at[dp]
    last[:, :W] = terms[:, :128] + terms[:, 128:256] + terms[:, 256:384] + terms[:, 384:]
    last[:, W:] = rows[:, ROWS:]
    last_start()
    h_v[...] = jnp.broadcast_to(lax.rsqrt(row_moment), (W, ROWS)).T
    col_scale = lax.rsqrt(column_moment)
    last_wait()
    totals = jnp.sum(lastbuf[...], axis=0)
    raw_total = jnp.sum(totals[:, :W], axis=1, keepdims=True)
    weight_total = jnp.sum(totals[:, W:], axis=1, keepdims=True)
    rms_update = jnp.sqrt(raw_total / (D * FF))
    shrink = 1.0 / jnp.maximum(1.0, rms_update / clip_level)
    rms_weight = jnp.sqrt(weight_total / (D * FF) + weight_eps)
    rate = learn_rate * rms_weight

    second_net = Net(send_sems, recv_sems)
    net.finish()

    def hidden_here(c):
        second_net.now += DOT_US
        product(xb, wb, c, h_v)
        nxt_v[:, c * W:(c + 1) * W] = h_v[...].astype(BF16)
        stores.append(pltpu.make_async_copy(
            nxt_v.at[:, pl.ds(c * W, W)], hidden.at[:, pl.ds(c * W, W)], local_sems.at[c]))
        stores[-1].start()

    stores = []
    second = GatherDp(second_net, me, wb, w_relay, hidden_here)
    for c in Y_FIRST + X_FIRST:
        cols = slice(c * W, (c + 1) * W)
        upd = g_v[c] * h_v[...] * (col_scale[:, cols] * shrink)
        u_v[:, cols] = upd
        fresh = w_v[:, cols] - rate * upd
        w_v[:, cols] = fresh
        block(wb, c, dp)[...] = fresh.astype(BF16)
        if c in Y_FIRST:
            second.along_y(c, False)
        second.along_x(c, 0, 0)
        second.along_x(c, 0, 1)
        if c in X_FIRST:
            second.along_y(c, False)
    stores.append(pltpu.make_async_copy(u_v, update, local_sems.at[8]))
    stores.append(pltpu.make_async_copy(w_v, new_weight, local_sems.at[9]))
    stores[0].start()
    stores[1].start()
    second_net.run()
    second_net.finish()
    for k in range(1, 8):
        to_z(k).wait_send()
        to_dp(k).wait_send()
    col_sent()
    row_sent()
    t_sent()
    last_sent()
    for copy in stores:
        copy.wait()


def body(activations, out_grads, weight, row_state, column_state, next_batch):
    any_space = pl.BlockSpec(memory_space=pl.ANY)
    vmem = pl.BlockSpec(memory_space=pltpu.VMEM)
    dma = pltpu.SemaphoreType.DMA
    new_weight, update, row_moment, column_moment, hidden = pl.pallas_call(
        kernel,
        name="adafactor",
        out_shape=(
            jax.ShapeDtypeStruct((ROWS, COLS), F32),
            jax.ShapeDtypeStruct((ROWS, COLS), F32),
            jax.ShapeDtypeStruct((1, ROWS), F32),
            jax.ShapeDtypeStruct((1, COLS), F32),
            jax.ShapeDtypeStruct((ROWS, COLS), BF16),
        ),
        in_specs=[any_space, any_space, any_space, vmem, vmem, any_space],
        out_specs=(any_space, any_space, vmem, vmem, any_space),
        scratch_shapes=[
            pltpu.VMEM((ROWS, W), BF16),
            pltpu.VMEM((ROWS, COLS), BF16),
            pltpu.VMEM((W, ROWS), BF16),
            pltpu.VMEM((8, 16, ROWS), BF16),
            pltpu.VMEM((ROWS, D), BF16),
            pltpu.VMEM((ROWS, D), BF16),
            pltpu.VMEM((CHUNKS, D, W), BF16),
            pltpu.VMEM((CHUNKS, D, W), BF16),
            pltpu.VMEM((RELAYS, ROWS // 2, W), BF16),
            pltpu.VMEM((RELAYS, ROWS // 2, W), BF16),
            pltpu.VMEM((ROWS, COLS), F32),
            pltpu.VMEM((CHUNKS, ROWS, W), F32),
            pltpu.VMEM((ROWS, COLS), F32),
            pltpu.VMEM((ROWS, W), F32),
            pltpu.VMEM((8, 1, COLS), F32),
            pltpu.VMEM((32, 1, ROWS + W), F32),
            pltpu.VMEM((32, 1, ROWS), F32),
            pltpu.VMEM((8, 1, 2 * W), F32),
            dma((COPIES,)), dma((COPIES,)),
            dma((8,)), dma((8,)), dma((8,)), dma((8,)),
            dma((8,)), dma((8,)), dma((32,)), dma((32,)),
            dma((32,)), dma((32,)), dma((8,)), dma((8,)),
            dma((11,)),
        ],
        compiler_params=pltpu.CompilerParams(
            collective_id=0, has_side_effects=True, vmem_limit_bytes=60 * 1024 * 1024),
    )(activations, out_grads, weight, row_state.reshape(1, ROWS), column_state.reshape(1, COLS), next_batch)
    return new_weight, update, row_moment.reshape(ROWS), column_moment.reshape(COLS), hidden


def solution(mesh):
    return jax.shard_map(
        body,
        mesh=mesh,
        in_specs=(P("dp", "mp"), P("dp", "mp"), P("dp", "mp"), P("dp"), P("mp"), P("dp", "mp")),
        out_specs=(P("dp", "mp"), P("dp", "mp"), P("dp"), P("mp"), P("dp", "mp")),
        check_vma=False,
    )
```

time: 578 us -> 188 us (0.33)
  waiting for transfers between devices: 381 us -> 0 us
  Pallas kernels: 0 us -> 181 us
  blocking collectives: 149 us -> 0 us
  matrix products: 19.5 us -> 0 us
  between operations: 15.2 us -> 0.66 us
  other arithmetic: 9.27 us -> 0 us
    reduce_scatter x1 -> x0, waiting for transfers between devices: 195 us -> none  [body(): lax.psum_scatter(lax.dot_general(block, out_grads, contract, preferred_el...]
    all_gather x3 -> x0, waiting for transfers between devices: 185 us -> none  [the longest x1 107 us: body(): lax.all_gather(weight_half, 'dp', axis=0, tiled=True)]
    pallas_call x0 -> x1, Pallas kernels: none -> 181 us  [body(): pl.pallas_call(kernel, name='adafactor', out_shape=(jax.ShapeDtypeStruct(...]
    psum x3 -> x0, blocking collectives: 149 us -> none  [the longest x1 78.4 us: body(): lax.psum((jnp.sum(raw_update * raw_update), jnp.sum(weight * weight)), ('...]
    dot_general x2 -> x0, matrix products: 19.5 us -> none  [the longest x1 10.4 us: body(): lax.dot_general(block, out_grads, contract, preferred_element_type=jnp.fl...]
  transfers between devices with their start and end apart: 4 -> 0, of which waited for: 3 -> 0; matrix products, arithmetic and copies ran while one was open for 2% -> 0% of each run, Pallas kernels for 0% -> 0%
where the time goes in v1:
time: 188 us
  Pallas kernels  181 us (96%)
  local copies, waits for them, and re-layouts  6.79 us (4%)
    pallas_call x1, Pallas kernels, body(): pl.pallas_call(kernel, name='adafactor', out_shape=(jax.ShapeDtypeStruct(...  181 us
    unnamed x13, local copies, waits for them, and re-layouts  6.79 us

profile of v1, /device:TPU:6, one launch (start us, length us, event | category | flops | bytes accessed | tf_op | source)
XLA Modules:
  0.0 188.4 jit_solution(13718994330704826149)
XLA Ops:
  0.6 180.9 %adafactor.1 = (f32[512,1024]{1,0:T(8,128)}, f32[512,1024]{1,0:T(8,128)}, f32[1,512]{1,0:T(1,128)}, f32[1,1024]{1,0:T(1,128)}, bf16[512,1024]{1,0:T(8,128)(2,1)}) custom-call(bf16[512,128]{1,0:T(8,128)(2,1)} %act.1, bf16[512,1024]{1,0:T(8,128)(2,1)} %out_grads.1, f32[512,1024]{1,0:T(8,128)} %weight.1, f32[1,512]{1,0:T(1,128)} %bitcast.6, f32[1,1024]{1,0:T(1,128)} %bitcast.4, ...), custom_call_target="tpu_custom_call" | custom-call | tf_op jit(solution)/shard_map/adafactor/pallas_call | solution.py:454
  181.6 0.0 copy-start
  181.6 3.3 %copy.16 = f32[512,1024]{1,0:T(8,128)} copy(f32[512,1024]{1,0:T(8,128)} %get-tuple-element.20) | data formatting | bytes 4194304
  184.9 0.0 copy-done
  184.9 0.0 copy-start.3
  184.9 0.0 copy-start.2
  184.9 0.0 copy-start.1
  184.9 1.3 copy.17
  186.2 0.0 copy-done.3
  186.2 0.6 copy.18
  186.8 0.0 copy-done.2
  186.8 0.6 copy.19
  187.4 0.0 copy-done.1
  187.4 1.0 copy.20
Async XLA Ops:
  181.6 3.3 %copy-start = (f32[512,1024]{1,0:T(8,128)S(1)}, f32[512,1024]{1,0:T(8,128)}, u32[]{:S(2)}) copy-start(f32[512,1024]{1,0:T(8,128)} %get-tuple-element.21) | copy-start | bytes 6291460
  184.9 1.3 copy-start.3
  184.9 1.9 %copy-start.2 = (f32[1,1024]{1,0:T(1,128)S(1)}, f32[1,1024]{1,0:T(1,128)}, u32[]{:S(2)}) copy-start(f32[1,1024]{1,0:T(1,128)} %get-tuple-element.13) | copy-start | bytes 12292
  184.9 2.5 %copy-start.1 = (bf16[512,1024]{1,0:T(8,128)(2,1)S(1)}, bf16[512,1024]{1,0:T(8,128)(2,1)}, u32[]{:S(2)}) copy-start(bf16[512,1024]{1,0:T(8,128)(2,1)} %get-tuple-element.24) | copy-start | bytes 3145732

commit v2 on v1

--- a/solution.py
+++ b/solution.py
@@ -28,7 +28,7 @@
 
 HOP_US = 1.7
 RATE = 46e3
-DOT_US = 1.6
+DOT_US = 0.2
 
 F32 = jnp.float32
 BF16 = jnp.bfloat16
@@ -60,6 +60,7 @@
         self.copies, self.heap, self.free = [], [], {}
         self.now = 0.0
         self.first = 0
+        self.idle = None
 
     def send(self, link, src, dst, device, size, then, hop=HOP_US):
         k = len(self.copies)
@@ -80,6 +81,10 @@
             copy.wait_recv()
             if then is not None:
                 then()
+            if self.idle is not None:
+                self.idle(2)
+        if self.idle is not None:
+            self.idle(1000)
 
     def finish(self):
         for copy in self.copies[self.first:]:
@@ -94,24 +99,38 @@
     return ref.at[c, pl.ds(pl.multiple_of(t * ROWS + half * rows, rows), rows), :]
 
 
+class Products:
+    def __init__(self, net, step, done):
+        self.net, self.step, self.done = net, step, done
+        self.queue, self.ready = [], False
+        self.left = {c: 16 for c in range(CHUNKS)}
+        net.idle = self.advance
+
+    def add(self, c, t, half=None):
+        self.queue.append((c, t, half))
+
+    def advance(self, count):
+        while self.ready and self.queue and count:
+            count -= 1
+            c, t, half = self.queue.pop(0)
+            self.step(c, t, half, self.left[c] == 16)
+            self.net.now += DOT_US if half is None else DOT_US / 2
+            self.left[c] -= 2 if half is None else 1
+            if self.left[c] == 0:
+                self.done(c)
+
+
 class GatherDp:
     FULL = ROWS * W * 2
 
-    def __init__(self, net, me, buf, relay, done):
-        self.net, self.me, self.buf, self.relay, self.done = net, me, buf, relay, done
-        self.left = {c: 10 for c in X_FIRST}
-        self.left.update({c: 12 for c in Y_FIRST})
+    def __init__(self, net, me, buf, relay, got):
+        self.net, self.me, self.buf, self.relay, self.got = net, me, buf, relay, got
         self.relays = 0
         self.partner_halves = {c: 0 for c in X_FIRST}
 
     def index(self, dy, other):
         xh = (self.me.xh + 1) % 2 if other else self.me.xh
         return 2 * ((self.me.y + dy) % 4) + xh
-
-    def got(self, c):
-        self.left[c] -= 1
-        if self.left[c] == 0:
-            self.done(c)
 
     def along_y(self, c, other):
         for sign in (1, -1):
@@ -127,12 +146,12 @@
         if c in Y_FIRST:
             self.along_x(c, -sign, 0)
             self.along_x(c, -sign, 1)
-        self.got(c)
+        self.got(c, self.index(-sign, other))
 
     def from_far_y(self, c, other, half):
         if c in Y_FIRST:
             self.along_x(c, 2, half)
-        self.got(c)
+        self.got(c, self.index(2, other), half)
 
     def along_x(self, c, dy, half):
         sign = 1 if half == 0 else -1
@@ -146,14 +165,14 @@
         xh = ((self.me.x + 4 - sign) % 4) // 2
         t = 2 * ((self.me.y + dy) % 4) + xh
         self.net.send(("x", sign), slot, block(self.buf, c, t, half), self.me.device(dx=sign),
-                      self.FULL // 2, functools.partial(self.from_x, c))
-
-    def from_x(self, c):
+                      self.FULL // 2, functools.partial(self.from_x, c, dy, half))
+
+    def from_x(self, c, dy, half):
         if c in X_FIRST:
             self.partner_halves[c] += 1
             if self.partner_halves[c] == 2:
                 self.along_y(c, True)
-        self.got(c)
+        self.got(c, self.index(dy, True), half)
 
 
 class GatherMp:
@@ -256,23 +275,29 @@
         to_z(k).start()
 
     net = Net(send_sems, recv_sems)
-    state = {"at": False, "ready": [], "count": 0}
+    state = {"count": 0}
     colbuf_row = colbuf.at[dp]
 
-    def product(left, right, c, out):
-        out[...] = jnp.zeros_like(out)
-
-        def step(k, carry):
-            s = pl.multiple_of(k * 512, 512)
-            out[...] += jnp.dot(left[:, pl.ds(s, 512)], right[c, pl.ds(s, 512), :],
-                                preferred_element_type=F32)
-            return carry
-
-        lax.fori_loop(0, 8, step, 0)
+    def product(left, right):
+        def step(c, t, half, first):
+            size = ROWS if half is None else ROWS // 2
+            s = pl.multiple_of(t * ROWS + (half or 0) * size, size)
+
+            def rows(k, carry):
+                r = pl.multiple_of(k * 256, 256)
+                part = jnp.dot(left[pl.ds(r, 256), pl.ds(s, size)], right[c, pl.ds(s, size), :],
+                               preferred_element_type=F32)
+                if first:
+                    g_v[c, pl.ds(r, 256), :] = part
+                else:
+                    g_v[c, pl.ds(r, 256), :] += part
+                return carry
+
+            lax.fori_loop(0, ROWS // 256, rows, 0)
+
+        return step
 
     def gradient(c):
-        net.now += DOT_US
-        product(at, ob, c, g_v.at[c])
         squares = g_v[c] * g_v[c] + tiny_square
         colbuf_row[:, pl.ds(c * W, W)] = jnp.sum(squares, axis=0, keepdims=True)
         if state["count"] == 0:
@@ -281,46 +306,10 @@
             h_v[...] += squares
         state["count"] += 1
 
-    def chunk_here(c):
-        if state["at"]:
-            gradient(c)
-        else:
-            state["ready"].append(c)
+    products = Products(net, product(at, ob), gradient)
 
     def at_here():
-        state["at"] = True
-        for c in state["ready"]:
-            gradient(c)
-
-    first = GatherDp(net, me, ob, o_relay, chunk_here)
-    for c in Y_FIRST:
-        loads[3 + c].wait()
-        first.along_y(c, False)
-        first.along_x(c, 0, 0)
-        first.along_x(c, 0, 1)
-    for k in range(1, 8):
-        to_z(k).wait_recv()
-    for k in range(1, 8):
-        to_dp(k).start()
-    at[pl.ds(strip_row, 16), pl.ds(pl.multiple_of(dp * ROWS, ROWS), ROWS)] = pieces[dp]
-    net.now = 5.0
-    for c in X_FIRST:
-        loads[3 + c].wait()
-        first.along_x(c, 0, 0)
-        first.along_x(c, 0, 1)
-        first.along_y(c, False)
-
-    def strip_x(z, xl, core):
-        return xb.at[:, pl.ds(pl.multiple_of((4 * z + 2 * xl + core) * W, W), W)]
-
-    def strip_a(z, xl, core):
-        return at.at[pl.ds(pl.multiple_of((2 * xl + core) * W + 16 * z, 16), 16), :]
-
-    for k in range(1, 8):
-        to_dp(k).wait_recv()
-    GatherMp(net, me, strip_a, {1: 4, -1: 3}, at_here).start()
-    loads[1].wait()
-    GatherMp(net, me, strip_x, {1: 3, -1: 4}, lambda: None).start()
+        products.ready = True
 
     loads[2].wait()
     wsq = jnp.zeros((8, 128), F32)
@@ -334,6 +323,35 @@
 
     wsq = lax.fori_loop(0, ROWS // 8, weight_step, wsq)
     wsum = jnp.sum(wsq, axis=0, keepdims=True)
+
+    first = GatherDp(net, me, ob, o_relay, products.add)
+    for k in range(1, 8):
+        to_z(k).wait_recv()
+    for k in range(1, 8):
+        to_dp(k).start()
+    at[pl.ds(strip_row, 16), pl.ds(pl.multiple_of(dp * ROWS, ROWS), ROWS)] = pieces[dp]
+    for c in Y_FIRST + X_FIRST:
+        loads[3 + c].wait()
+        products.add(c, dp)
+        if c in Y_FIRST:
+            first.along_y(c, False)
+        first.along_x(c, 0, 0)
+        first.along_x(c, 0, 1)
+        if c in X_FIRST:
+            first.along_y(c, False)
+    net.now = 5.0
+
+    def strip_x(z, xl, core):
+        return xb.at[:, pl.ds(pl.multiple_of((4 * z + 2 * xl + core) * W, W), W)]
+
+    def strip_a(z, xl, core):
+        return at.at[pl.ds(pl.multiple_of((2 * xl + core) * W + 16 * z, 16), 16), :]
+
+    for k in range(1, 8):
+        to_dp(k).wait_recv()
+    GatherMp(net, me, strip_a, {1: 4, -1: 3}, at_here).start()
+    loads[1].wait()
+    GatherMp(net, me, strip_x, {1: 3, -1: 4}, lambda: None).start()
 
     net.run()
 
@@ -408,15 +426,14 @@
     net.finish()
 
     def hidden_here(c):
-        second_net.now += DOT_US
-        product(xb, wb, c, h_v)
-        nxt_v[:, c * W:(c + 1) * W] = h_v[...].astype(BF16)
+        nxt_v[:, c * W:(c + 1) * W] = g_v[c].astype(BF16)
         stores.append(pltpu.make_async_copy(
             nxt_v.at[:, pl.ds(c * W, W)], hidden.at[:, pl.ds(c * W, W)], local_sems.at[c]))
         stores[-1].start()
 
     stores = []
-    second = GatherDp(second_net, me, wb, w_relay, hidden_here)
+    products = Products(second_net, product(xb, wb), hidden_here)
+    second = GatherDp(second_net, me, wb, w_relay, products.add)
     for c in Y_FIRST + X_FIRST:
         cols = slice(c * W, (c + 1) * W)
         upd = g_v[c] * h_v[...] * (col_scale[:, cols] * shrink)
@@ -424,6 +441,7 @@
         fresh = w_v[:, cols] - rate * upd
         w_v[:, cols] = fresh
         block(wb, c, dp)[...] = fresh.astype(BF16)
+        products.add(c, dp)
         if c in Y_FIRST:
             second.along_y(c, False)
         second.along_x(c, 0, 0)
@@ -434,6 +452,7 @@
     stores.append(pltpu.make_async_copy(w_v, new_weight, local_sems.at[9]))
     stores[0].start()
     stores[1].start()
+    products.ready = True
     second_net.run()
     second_net.finish()
     for k in range(1, 8):

time: 188 us -> 199 us (1.059)
  Pallas kernels: 181 us -> 192 us
    pallas_call x1, Pallas kernels: 181 us -> 192 us  [body(): pl.pallas_call(kernel, name='adafactor', out_shape=(jax.ShapeDtypeStruct(...]
where the time goes in v2:
time: 199 us
  Pallas kernels  192 us (96%)
  local copies, waits for them, and re-layouts  6.79 us (3%)
    pallas_call x1, Pallas kernels, body(): pl.pallas_call(kernel, name='adafactor', out_shape=(jax.ShapeDtypeStruct(...  192 us
    unnamed x13, local copies, waits for them, and re-layouts  6.79 us

profile of v2, /device:TPU:6, one launch (start us, length us, event | category | flops | bytes accessed | tf_op | source)
XLA Modules:
  0.0 199.0 jit_solution(12396880258902112485)
XLA Ops:
  0.6 191.5 %adafactor.1 = (f32[512,1024]{1,0:T(8,128)}, f32[512,1024]{1,0:T(8,128)}, f32[1,512]{1,0:T(1,128)}, f32[1,1024]{1,0:T(1,128)}, bf16[512,1024]{1,0:T(8,128)(2,1)}) custom-call(bf16[512,128]{1,0:T(8,128)(2,1)} %act.1, bf16[512,1024]{1,0:T(8,128)(2,1)} %out_grads.1, f32[512,1024]{1,0:T(8,128)} %weight.1, f32[1,512]{1,0:T(1,128)} %bitcast.6, f32[1,1024]{1,0:T(1,128)} %bitcast.4, ...), custom_call_target="tpu_custom_call" | custom-call | tf_op jit(solution)/shard_map/adafactor/pallas_call | solution.py:473
  192.2 0.0 copy-start
  192.2 3.3 %copy.16 = f32[512,1024]{1,0:T(8,128)} copy(f32[512,1024]{1,0:T(8,128)} %get-tuple-element.20) | data formatting | bytes 4194304
  195.5 0.0 copy-done
  195.5 0.0 copy-start.3
  195.5 0.0 copy-start.2
  195.5 0.0 copy-start.1
  195.5 1.3 copy.17
  196.8 0.0 copy-done.3
  196.8 0.6 copy.18
  197.4 0.0 copy-done.2
  197.4 0.6 copy.19
  198.0 0.0 copy-done.1
  198.0 1.0 copy.20
Async XLA Ops:
  192.2 3.3 %copy-start = (f32[512,1024]{1,0:T(8,128)S(1)}, f32[512,1024]{1,0:T(8,128)}, u32[]{:S(2)}) copy-start(f32[512,1024]{1,0:T(8,128)} %get-tuple-element.21) | copy-start | bytes 6291460
  195.5 1.3 copy-start.3
  195.5 1.9 copy-start.2
  195.5 2.5 %copy-start.1 = (bf16[512,1024]{1,0:T(8,128)(2,1)S(1)}, bf16[512,1024]{1,0:T(8,128)(2,1)}, u32[]{:S(2)}) copy-start(bf16[512,1024]{1,0:T(8,128)(2,1)} %get-tuple-element.24) | copy-start | bytes 3145732
